TPU v7x, 32 devices: a whole 2x2x4 slice. The times are simulated.
32 devices in a mesh: region: 16 (over z, x, core), sub: 2 (over y).
Axes of the slice: x: 2, y: 2, z: 4, core: 2. Of those that a mesh axis runs over, the one named last changes fastest.
Arguments:
- source: float32 [8, 8, 8, 8192], P(None, None, None, ('region', 'sub')), may hold values from -3.5 to 4.5
- metric: float32 [3, 8, 8, 8, 8192], P(None, None, None, None, ('region', 'sub')), may hold values from 0.002 to 0.008
- face_area: float32 [6, 8192], P(None, ('region', 'sub')), may hold values from 0.5 to 13.5
- outlet_gain: float32 [8], replicated, may hold values from 0.0018310547 to 0.0073242188
- neighbour: int32 [6, 8192], P(None, ('region', 'sub')), may hold values from 0 to 2048, as said below
- orient: int32 [6, 8192], P(None, ('region', 'sub')), may hold values from 0 to 7
- outlet: int32 [6, 8192], P(None, ('region', 'sub')), may hold values from 0 to 8, as said below
- export_list: int32 [128, 128], P(('region', 'sub')), may hold values from 0 to 1535, as said below
Outputs:
- solution: float32 [8, 8, 8, 8192], P(None, None, None, ('region', 'sub'))
- residual: float32 [8, 8, 8, 8192], P(None, None, None, ('region', 'sub'))
Inputs may be any that keep to these rules, and one draw needn't show every extreme that they name: Values below 1536 name the device's own faces, the next 128 each the four received lists in pool order; 2048 means the face has no neighbour, as on every outlet face and for any list from a device outside the mesh. 8 means the face belongs to no outlet. `export_list`: each row holds 128 different local face numbers.
All inputs are finite; a program needn't handle non-finite values.
Results may differ from a plain program's by a relative error of at most 0.0001.
Values sent between devices are 32-bit elements; how exact they have to be, the bound alone decides.
A program may use at most 64 MiB of HBM per device.

v0:
```python
import jax
import jax.numpy as jnp
import numpy as np
from jax import lax
from jax.sharding import PartitionSpec as P

NP = 8
OUTLETS = 8
ITERS = 4
GLL_POINTS = np.array(
    [
        -1.0,
        -0.8717401485096066,
        -0.5917001814331423,
        -0.2092992179024789,
        0.2092992179024789,
        0.5917001814331423,
        0.8717401485096066,
        1.0,
    ]
)


def extended(x, sides, width):
    for axis, dim in sides:
        devices, length = (lax.axis_size(axis), x.shape[dim])
        up = [(i, (i + 1) % devices) for i in range(devices - 1)]
        down = [(j, i) for i, j in up]
        last = lax.slice_in_dim(x, length - width, length, axis=dim)
        first = lax.slice_in_dim(x, 0, width, axis=dim)
        before = lax.ppermute(last, axis, up)
        after = lax.ppermute(first, axis, down)
        x = jnp.concatenate([before, x, after], axis=dim)
    return x


def legendre_seven(points):
    previous = points * 0.0 + 1.0
    current = points * 1.0
    for degree in range(1, 7):
        previous, current = (
            current,
            ((2 * degree + 1) * points * current - degree * previous) / (degree + 1),
        )
    return current


def node_tables():
    values = legendre_seven(GLL_POINTS)
    weights = 2.0 / (56.0 * values * values)
    equal = (GLL_POINTS[:, None] == GLL_POINTS[None, :]) * 1.0
    differ = GLL_POINTS[:, None] - GLL_POINTS[None, :] + equal
    deriv = values[:, None] / (values[None, :] * differ) * (1.0 - equal)
    deriv[0, 0] = -14.0
    deriv[7, 7] = 14.0
    return (deriv, np.outer(weights, weights).reshape(-1))


def select_table():
    table = np.zeros((6, NP * NP, NP * NP * NP))
    for first in range(NP):
        for second in range(NP):
            slot = first * NP + second
            table[0, slot, 0 * NP * NP + first * NP + second] = 1.0
            table[1, slot, (NP - 1) * NP * NP + first * NP + second] = 1.0
            table[2, slot, first * NP * NP + 0 * NP + second] = 1.0
            table[3, slot, first * NP * NP + (NP - 1) * NP + second] = 1.0
            table[4, slot, first * NP * NP + second * NP + 0] = 1.0
            table[5, slot, first * NP * NP + second * NP + NP - 1] = 1.0
    return table


def turn_table():
    table = np.zeros((8, NP * NP, NP * NP))
    for variant in range(8):
        moved = np.arange(NP * NP).reshape(NP, NP)
        if variant & 1:
            moved = moved[::-1, :]
        if variant & 2:
            moved = moved[:, ::-1]
        if variant & 4:
            moved = moved.T
        flat_moved = moved.reshape(-1)
        for place in range(NP * NP):
            table[variant, place, flat_moved[place]] = 1.0
    return table


def stiffness(field, metric, deriv):
    highest = lax.Precision.HIGHEST
    grad_a = jnp.einsum("ai,ijke->ajke", deriv, field, precision=highest)
    grad_b = jnp.einsum("bj,ijke->ibke", deriv, field, precision=highest)
    grad_c = jnp.einsum("ck,ijke->ijce", deriv, field, precision=highest)
    result = jnp.einsum("ai,ajke->ijke", deriv, metric[0] * grad_a, precision=highest)
    result = result + jnp.einsum("bj,ibke->ijke", deriv, metric[1] * grad_b, precision=highest)
    return result + jnp.einsum("ck,ijce->ijke", deriv, metric[2] * grad_c, precision=highest)


def local_diagonal(metric, deriv):
    highest = lax.Precision.HIGHEST
    square = deriv * deriv
    result = jnp.einsum("ai,ajke->ijke", square, metric[0], precision=highest)
    result = result + jnp.einsum("bj,ibke->ijke", square, metric[1], precision=highest)
    return result + jnp.einsum("ck,ijce->ijke", square, metric[2], precision=highest)


def face_matrix(field, selector):
    flat_field = field.reshape(NP * NP * NP, -1)
    picked = jnp.einsum("fqn,ne->qfe", selector, flat_field, precision=lax.Precision.HIGHEST)
    return picked.reshape(NP * NP, -1)


def add_faces(field, blocks, selector):
    elem_count = field.shape[3]
    grouped = blocks.reshape(NP * NP, 6, elem_count)
    spread = jnp.einsum("fqn,qfe->ne", selector, grouped, precision=lax.Precision.HIGHEST)
    return field + spread.reshape(field.shape)


def received_blocks(sent_faces, slot_count):
    sub_ext = extended(sent_faces[:, : 2 * slot_count], (("sub", 1),), slot_count)
    region_ext = extended(sent_faces[:, 2 * slot_count :], (("region", 1),), slot_count)
    return [
        sub_ext[:, :slot_count],
        sub_ext[:, 3 * slot_count :],
        region_ext[:, :slot_count],
        region_ext[:, 3 * slot_count :],
    ]


def assemble(values, links, code_hits, rows, slot_count, selector, turner):
    own_faces = face_matrix(values, selector)
    sent_faces = jnp.take(own_faces, rows, axis=1)
    arrived = received_blocks(sent_faces, slot_count)
    face_pool = jnp.concatenate([own_faces] + arrived, axis=1)
    limit = face_pool.shape[1]
    fetched = jnp.take(face_pool, jnp.minimum(links, limit - 1), axis=1)
    fetched = jnp.where(links[None, :] < limit, fetched, 0.0)
    variants = jnp.einsum("vpq,qx->vpx", turner, fetched, precision=lax.Precision.HIGHEST)
    turned = jnp.sum(variants * code_hits[:, None, :], axis=0)
    return add_faces(values, turned, selector)


def outlet_totals(direction, weights, area_flat, outlet_hits, selector):
    sums = jnp.dot(weights, face_matrix(direction, selector), precision=lax.Precision.HIGHEST)
    partial_value = jnp.dot(outlet_hits, area_flat * sums, precision=lax.Precision.HIGHEST)
    return lax.psum(partial_value, ("region", "sub"))


def add_outlet(values, totals, weights, area_flat, outlet_hits, outlet_gain, selector):
    coeff = jnp.dot(outlet_gain * totals, outlet_hits, precision=lax.Precision.HIGHEST) * area_flat
    extra = weights[:, None] * coeff[None, :]
    return add_faces(values, extra, selector)


def per_device(source, metric, face_area, outlet_gain, neighbour, orient, outlet, export_list):
    deriv_np, weights_np = node_tables()
    deriv = jnp.asarray(deriv_np, jnp.float32)
    weights = jnp.asarray(weights_np, jnp.float32)
    selector = jnp.asarray(select_table(), jnp.float32)
    turner = jnp.asarray(turn_table(), jnp.float32)
    links = neighbour.reshape(-1)
    variant_ids = jnp.arange(8, dtype=jnp.int32)
    code_hits = (orient.reshape(-1)[None, :] == variant_ids[:, None]).astype(jnp.float32)
    rows = export_list.reshape(-1)
    slot_count = export_list.shape[1]
    area_flat = face_area.reshape(-1)
    outlet_ids = jnp.arange(OUTLETS, dtype=jnp.int32)
    outlet_hits = (outlet.reshape(-1)[None, :] == outlet_ids[:, None]).astype(jnp.float32)
    diagonal = assemble(
        local_diagonal(metric, deriv), links, code_hits, rows, slot_count, selector, turner
    )
    inverse = 1.0 / diagonal
    centre = 4.5
    half_width = 3.5
    ratio = centre / half_width
    rho_prev = 1.0 / ratio
    residual = source
    direction = inverse * residual / centre
    solution = jnp.zeros_like(source)
    for sweep in range(ITERS):
        solution = solution + direction
        image = assemble(
            stiffness(direction, metric, deriv),
            links,
            code_hits,
            rows,
            slot_count,
            selector,
            turner,
        )
        totals = outlet_totals(direction, weights, area_flat, outlet_hits, selector)
        residual = residual - add_outlet(
            image, totals, weights, area_flat, outlet_hits, outlet_gain, selector
        )
        rho_next = 1.0 / (2.0 * ratio - rho_prev)
        direction = (
            rho_next * rho_prev * direction + 2.0 * rho_next / half_width * inverse * residual
        )
        rho_prev = rho_next
    solution = solution + direction
    return (solution, residual)


def solution(mesh):
    placed = (
        P(None, None, None, ("region", "sub")),
        P(None, None, None, None, ("region", "sub")),
        P(None, ("region", "sub")),
        P(),
        P(None, ("region", "sub")),
        P(None, ("region", "sub")),
        P(None, ("region", "sub")),
        P(("region", "sub"), None),
    )
    return jax.shard_map(
        per_device,
        mesh=mesh,
        in_specs=placed,
        out_specs=(P(None, None, None, ("region", "sub")), P(None, None, None, ("region", "sub"))),
        check_vma=False,
    )
```

profile of v0, /device:TPU:0, one launch (start us, length us, event | category | flops | bytes accessed | tf_op | source)
XLA Modules:
  0.0 406.7 jit_solution(18317932855639597581)
XLA Ops:
  10.7 4.9 %collective-permute-start = (f32[64,128]{0,1:T(8,128)S(1)}, f32[64,128]{0,1:T(8,128)S(1)}, u32[]{:S(2)}, u32[]{:S(2)}) collective-permute-start(f32[64,128]{0,1:T(8,128)S(1)} %get-tuple-element.39), channel_id=1, source_target_pairs={{0,1},{2,3},{4,5},{6,7},{8,9},{10,11},{12,13},{14,15},{16,17},{18,... | collective-permute-start | bytes 98312 | tf_op jit(solution)/shard_map/ppermute | solution.py:31
  23.1 3.7 gather_fusion.1
  26.8 4.3 %fusion = f32[64,1536]{1,0:T(8,128)S(1)} fusion(f32[8,1536]{1,0:T(8,128)S(1)} %fusion.93, f32[8,64,64]{2,1,0:T(8,128)} %constant.59.clone, f32[1536,64]{1,0:T(8,128)} %gather_fusion.1, pred[1536]{0:T(1024)(128)(4,1)S(1)} %compare_and_fusion, pred[1536]{0:T(1024)(128)(4,1)S(1)} %lt.28), kind=kOutput, calls=%fused_computation.15 | convolution fusion | flops 605650944 | bytes 969728 | tf_op jit(solution)/shard_map/vpq,qx->vpx/dot_general | solution.py:139
  48.0 16.7 %collective-permute-start.4 = (f32[64,128]{0,1:T(8,128)}, f32[64,128]{0,1:T(8,128)}, u32[]{:S(2)}, u32[]{:S(2)}) collective-permute-start(f32[64,128]{0,1:T(8,128)} %get-tuple-element.35), channel_id=1, source_target_pairs={{0,1},{2,3},{4,5},{6,7},{8,9},{10,11},{12,13},{14,15},{16,17},{18,... | collective-permute-start | bytes 98312 | tf_op jit(solution)/shard_map/ppermute | solution.py:31
  65.9 4.6 %collective-permute-start.6 = (f32[64,128]{0,1:T(8,128)}, f32[64,128]{0,1:T(8,128)S(1)}, u32[]{:S(2)}, u32[]{:S(2)}) collective-permute-start(f32[64,128]{0,1:T(8,128)} %get-tuple-element.33), channel_id=1, source_target_pairs={{0,2},{2,4},{4,6},{6,8},{8,10},{10,12},{12,14},{14,16},{16,18},{18... | collective-permute-start | bytes 98312 | tf_op jit(solution)/shard_map/ppermute | solution.py:31
  74.3 44.2 %psum.28 = f32[8]{0:T(128)S(1)} all-reduce(f32[8]{0:T(128)S(1)} %convolution_bitcast_fusion.20), channel_id=1, replica_groups=mesh['region'=16,'sub'=2] {'region','sub'}, use_global_device_ids=true, to_apply=%region_2.5 | all-reduce | flops 8 | bytes 64 | tf_op jit(solution)/shard_map/psum | solution.py:147
  123.5 3.7 gather_fusion.3
  127.3 4.3 %fusion.1 = f32[64,1536]{1,0:T(8,128)S(1)} fusion(f32[8,1536]{1,0:T(8,128)S(1)} %copy-done.38, f32[8,64,64]{2,1,0:T(8,128)} %constant.59.clone, f32[1536,64]{1,0:T(8,128)} %gather_fusion.3, pred[1536]{0:T(1024)(128)(4,1)S(1)} %copy-done.60, pred[1536]{0:T(1024)(128)(4,1)S(1)} %copy-done.65), kind=kOutput, calls=%fused_computation.16 | convolution fusion | flops 605650944 | bytes 969728 | tf_op jit(solution)/shard_map/vpq,qx->vpx/dot_general | solution.py:139
  145.6 2.8 gather_fusion.4
  150.2 4.9 %collective-permute-start.8 = (f32[64,128]{0,1:T(8,128)}, f32[64,128]{0,1:T(8,128)}, u32[]{:S(2)}, u32[]{:S(2)}) collective-permute-start(f32[64,128]{0,1:T(8,128)} %get-tuple-element.31), channel_id=1, source_target_pairs={{0,1},{2,3},{4,5},{6,7},{8,9},{10,11},{12,13},{14,15},{16,17},{18,... | collective-permute-start | bytes 98312 | tf_op jit(solution)/shard_map/ppermute | solution.py:31
  160.8 45.4 %psum.29 = f32[8]{0:T(128)S(1)} all-reduce(f32[8]{0:T(128)S(1)} %convolution_bitcast_fusion.19), channel_id=1, replica_groups=mesh['region'=16,'sub'=2] {'region','sub'}, use_global_device_ids=true, to_apply=%region_4.7 | all-reduce | flops 8 | bytes 64 | tf_op jit(solution)/shard_map/psum | solution.py:147
  207.1 3.0 fusion.66
  215.2 4.9 %gather_fusion.5 = f32[1536,64]{1,0:T(8,128)} fusion(f32[64,2048]{0,1:T(8,128)} %constant_dynamic-update-slice_fusion.10, s32[2048]{0:T(1024)S(1)} %pad_clamp_fusion), kind=kCustom, calls=%fused_computation.7.clone | custom fusion | bytes 792576 | tf_op jit(solution)/shard_map/jit(_take)/gather | solution.py:137
  220.1 4.3 %fusion.2 = f32[64,1536]{1,0:T(8,128)S(1)} fusion(f32[8,1536]{1,0:T(8,128)S(1)} %copy-done.38, f32[8,64,64]{2,1,0:T(8,128)} %constant.59.clone, f32[1536,64]{1,0:T(8,128)} %gather_fusion.5, pred[1536]{0:T(1024)(128)(4,1)S(1)} %copy-done.61, pred[1536]{0:T(1024)(128)(4,1)S(1)} %copy-done.66), kind=kOutput, calls=%fused_computation.17 | convolution fusion | flops 605650944 | bytes 969728 | tf_op jit(solution)/shard_map/vpq,qx->vpx/dot_general | solution.py:139
  239.0 2.8 gather_fusion.6
  243.6 4.9 %collective-permute-start.12 = (f32[64,128]{0,1:T(8,128)}, f32[64,128]{0,1:T(8,128)}, u32[]{:S(2)}, u32[]{:S(2)}) collective-permute-start(f32[64,128]{0,1:T(8,128)} %get-tuple-element.27), channel_id=1, source_target_pairs={{0,1},{2,3},{4,5},{6,7},{8,9},{10,11},{12,13},{14,15},{16,17},{18,... | collective-permute-start | bytes 98312 | tf_op jit(solution)/shard_map/ppermute | solution.py:31
  255.6 43.6 %psum.30 = f32[8]{0:T(128)} all-reduce(f32[8]{0:T(128)} %convolution_bitcast_fusion.18), channel_id=1, replica_groups=mesh['region'=16,'sub'=2] {'region','sub'}, use_global_device_ids=true, to_apply=%region_6.9 | all-reduce | flops 8 | bytes 64 | tf_op jit(solution)/shard_map/psum | solution.py:147
  309.6 4.9 %gather_fusion.7 = f32[1536,64]{1,0:T(8,128)} fusion(f32[64,2048]{0,1:T(8,128)} %constant_dynamic-update-slice_fusion.15, s32[2048]{0:T(1024)S(1)} %pad_clamp_fusion), kind=kCustom, calls=%fused_computation.8.clone | custom fusion | bytes 792576 | tf_op jit(solution)/shard_map/jit(_take)/gather | solution.py:137
  314.5 4.3 %fusion.3 = f32[64,1536]{1,0:T(8,128)S(1)} fusion(f32[8,1536]{1,0:T(8,128)S(1)} %copy-done.38, f32[8,64,64]{2,1,0:T(8,128)} %constant.59.clone, f32[1536,64]{1,0:T(8,128)} %gather_fusion.7, pred[1536]{0:T(1024)(128)(4,1)S(1)} %copy-done.62, pred[1536]{0:T(1024)(128)(4,1)S(1)} %copy-done.67), kind=kOutput, calls=%fused_computation.18 | convolution fusion | flops 605650944 | bytes 969728 | tf_op jit(solution)/shard_map/vpq,qx->vpx/dot_general | solution.py:139
  333.3 5.1 %collective-permute-start.16 = (f32[64,128]{0,1:T(8,128)}, f32[64,128]{0,1:T(8,128)}, u32[]{:S(2)}, u32[]{:S(2)}) collective-permute-start(f32[64,128]{0,1:T(8,128)} %get-tuple-element.23), channel_id=1, source_target_pairs={{0,1},{2,3},{4,5},{6,7},{8,9},{10,11},{12,13},{14,15},{16,17},{18,... | collective-permute-start | bytes 98312 | tf_op jit(solution)/shard_map/ppermute | solution.py:31
  345.0 44.7 %psum.31 = f32[8]{0:T(128)S(1)} all-reduce(f32[8]{0:T(128)S(1)} %convolution_bitcast_fusion.17), channel_id=1, replica_groups=mesh['region'=16,'sub'=2] {'region','sub'}, use_global_device_ids=true, to_apply=%region_8.11 | all-reduce | flops 8 | bytes 64 | tf_op jit(solution)/shard_map/psum | solution.py:147
  389.9 2.3 fusion.62
  394.0 3.7 gather_fusion.9
  397.7 4.3 %fusion.4 = f32[64,1536]{1,0:T(8,128)S(1)} fusion(f32[8,1536]{1,0:T(8,128)S(1)} %copy-done.39, f32[8,64,64]{2,1,0:T(8,128)} %constant.59.clone, f32[1536,64]{1,0:T(8,128)} %gather_fusion.9, pred[1536]{0:T(1024)(128)(4,1)S(1)} %copy-done.63, pred[1536]{0:T(1024)(128)(4,1)S(1)} %copy-done.68), kind=kOutput, calls=%fused_computation.19 | convolution fusion | flops 605650944 | bytes 969728 | tf_op jit(solution)/shard_map/vpq,qx->vpx/dot_general | solution.py:139
  (325 shorter events, 132.1 us)
Async XLA Ops:
  10.7 11.4 %collective-permute-start = (f32[64,128]{0,1:T(8,128)S(1)}, f32[64,128]{0,1:T(8,128)S(1)}, u32[]{:S(2)}, u32[]{:S(2)}) collective-permute-start(f32[64,128]{0,1:T(8,128)S(1)} %get-tuple-element.39), channel_id=1, source_target_pairs={{0,1},{2,3},{4,5},{6,7},{8,9},{10,11},{12,13},{14,15},{16,17},{18,... | collective-permute-start | bytes 98312 | tf_op jit(solution)/shard_map/ppermute | solution.py:31
  15.6 6.5 %collective-permute-start.1 = (f32[64,128]{0,1:T(8,128)S(1)}, f32[64,128]{0,1:T(8,128)S(1)}, u32[]{:S(2)}, u32[]{:S(2)}) collective-permute-start(f32[64,128]{0,1:T(8,128)S(1)} %get-tuple-element.38), channel_id=1, source_target_pairs={{1,0},{3,2},{5,4},{7,6},{9,8},{11,10},{13,12},{15,14},{17,16},{19,... | collective-permute-start | bytes 98312 | tf_op jit(solution)/shard_map/ppermute | solution.py:32
  16.9 5.2 %collective-permute-start.2 = (f32[64,128]{0,1:T(8,128)S(1)}, f32[64,128]{0,1:T(8,128)S(1)}, u32[]{:S(2)}, u32[]{:S(2)}) collective-permute-start(f32[64,128]{0,1:T(8,128)S(1)} %get-tuple-element.37), channel_id=1, source_target_pairs={{0,2},{2,4},{4,6},{6,8},{8,10},{10,12},{12,14},{14,16},{16,18},{18... | collective-permute-start | bytes 98312 | tf_op jit(solution)/shard_map/ppermute | solution.py:31
  18.4 4.7 %collective-permute-start.3 = (f32[64,128]{0,1:T(8,128)S(1)}, f32[64,128]{0,1:T(8,128)S(1)}, u32[]{:S(2)}, u32[]{:S(2)}) collective-permute-start(f32[64,128]{0,1:T(8,128)S(1)} %get-tuple-element.36), channel_id=1, source_target_pairs={{2,0},{4,2},{6,4},{8,6},{10,8},{12,10},{14,12},{16,14},{18,16},{20... | collective-permute-start | bytes 98312 | tf_op jit(solution)/shard_map/ppermute | solution.py:32
  48.0 70.4 %copy-start.69 = (f32[8]{0:T(128)S(1)}, f32[8]{0:T(128)}, u32[]{:S(2)}) copy-start(f32[8]{0:T(128)} %param.19) | copy-start | bytes 100
  48.0 70.6 %copy-start.45 = (f32[64]{0:T(128)S(1)}, f32[64]{0:T(128)}, u32[]{:S(2)}) copy-start(f32[64]{0:T(128)} %constant.32.clone) | copy-start | bytes 772
  48.0 73.0 %collective-permute-start.4 = (f32[64,128]{0,1:T(8,128)}, f32[64,128]{0,1:T(8,128)}, u32[]{:S(2)}, u32[]{:S(2)}) collective-permute-start(f32[64,128]{0,1:T(8,128)} %get-tuple-element.35), channel_id=1, source_target_pairs={{0,1},{2,3},{4,5},{6,7},{8,9},{10,11},{12,13},{14,15},{16,17},{18,... | collective-permute-start | bytes 98312 | tf_op jit(solution)/shard_map/ppermute | solution.py:31
  64.6 57.2 %collective-permute-start.5 = (f32[64,128]{0,1:T(8,128)}, f32[64,128]{0,1:T(8,128)}, u32[]{:S(2)}, u32[]{:S(2)}) collective-permute-start(f32[64,128]{0,1:T(8,128)} %get-tuple-element.34), channel_id=1, source_target_pairs={{1,0},{3,2},{5,4},{7,6},{9,8},{11,10},{13,12},{15,14},{17,16},{19,... | collective-permute-start | bytes 98312 | tf_op jit(solution)/shard_map/ppermute | solution.py:32
  65.9 56.7 %collective-permute-start.6 = (f32[64,128]{0,1:T(8,128)}, f32[64,128]{0,1:T(8,128)S(1)}, u32[]{:S(2)}, u32[]{:S(2)}) collective-permute-start(f32[64,128]{0,1:T(8,128)} %get-tuple-element.33), channel_id=1, source_target_pairs={{0,2},{2,4},{4,6},{6,8},{8,10},{10,12},{12,14},{14,16},{16,18},{18... | collective-permute-start | bytes 98312 | tf_op jit(solution)/shard_map/ppermute | solution.py:31
  72.9 49.7 %collective-permute-start.7 = (f32[64,128]{0,1:T(8,128)}, f32[64,128]{0,1:T(8,128)}, u32[]{:S(2)}, u32[]{:S(2)}) collective-permute-start(f32[64,128]{0,1:T(8,128)} %get-tuple-element.32), channel_id=1, source_target_pairs={{2,0},{4,2},{6,4},{8,6},{10,8},{12,10},{14,12},{16,14},{18,16},{20... | collective-permute-start | bytes 98312 | tf_op jit(solution)/shard_map/ppermute | solution.py:32
  150.2 60.8 %collective-permute-start.8 = (f32[64,128]{0,1:T(8,128)}, f32[64,128]{0,1:T(8,128)}, u32[]{:S(2)}, u32[]{:S(2)}) collective-permute-start(f32[64,128]{0,1:T(8,128)} %get-tuple-element.31), channel_id=1, source_target_pairs={{0,1},{2,3},{4,5},{6,7},{8,9},{10,11},{12,13},{14,15},{16,17},{18,... | collective-permute-start | bytes 98312 | tf_op jit(solution)/shard_map/ppermute | solution.py:31
  155.1 57.4 %collective-permute-start.9 = (f32[64,128]{0,1:T(8,128)}, f32[64,128]{0,1:T(8,128)}, u32[]{:S(2)}, u32[]{:S(2)}) collective-permute-start(f32[64,128]{0,1:T(8,128)} %get-tuple-element.30), channel_id=1, source_target_pairs={{1,0},{3,2},{5,4},{7,6},{9,8},{11,10},{13,12},{15,14},{17,16},{19,... | collective-permute-start | bytes 98312 | tf_op jit(solution)/shard_map/ppermute | solution.py:32
  156.4 57.5 %collective-permute-start.10 = (f32[64,128]{0,1:T(8,128)}, f32[64,128]{0,1:T(8,128)S(1)}, u32[]{:S(2)}, u32[]{:S(2)}) collective-permute-start(f32[64,128]{0,1:T(8,128)} %get-tuple-element.29), channel_id=1, source_target_pairs={{0,2},{2,4},{4,6},{6,8},{8,10},{10,12},{12,14},{14,16},{16,18},{18... | collective-permute-start | bytes 98312 | tf_op jit(solution)/shard_map/ppermute | solution.py:31
  159.5 55.1 %collective-permute-start.11 = (f32[64,128]{0,1:T(8,128)}, f32[64,128]{0,1:T(8,128)S(1)}, u32[]{:S(2)}, u32[]{:S(2)}) collective-permute-start(f32[64,128]{0,1:T(8,128)} %get-tuple-element.28), channel_id=1, source_target_pairs={{2,0},{4,2},{6,4},{8,6},{10,8},{12,10},{14,12},{16,14},{18,16},{20... | collective-permute-start | bytes 98312 | tf_op jit(solution)/shard_map/ppermute | solution.py:32
  243.6 57.8 %copy-start.46 = (f32[64]{0:T(128)S(1)}, f32[64]{0:T(128)}, u32[]{:S(2)}) copy-start(f32[64]{0:T(128)} %constant.32.clone) | copy-start | bytes 772
  243.6 61.0 %collective-permute-start.12 = (f32[64,128]{0,1:T(8,128)}, f32[64,128]{0,1:T(8,128)}, u32[]{:S(2)}, u32[]{:S(2)}) collective-permute-start(f32[64,128]{0,1:T(8,128)} %get-tuple-element.27), channel_id=1, source_target_pairs={{0,1},{2,3},{4,5},{6,7},{8,9},{10,11},{12,13},{14,15},{16,17},{18,... | collective-permute-start | bytes 98312 | tf_op jit(solution)/shard_map/ppermute | solution.py:31
  248.5 57.5 %collective-permute-start.13 = (f32[64,128]{0,1:T(8,128)}, f32[64,128]{0,1:T(8,128)}, u32[]{:S(2)}, u32[]{:S(2)}) collective-permute-start(f32[64,128]{0,1:T(8,128)} %get-tuple-element.26), channel_id=1, source_target_pairs={{1,0},{3,2},{5,4},{7,6},{9,8},{11,10},{13,12},{15,14},{17,16},{19,... | collective-permute-start | bytes 98312 | tf_op jit(solution)/shard_map/ppermute | solution.py:32
  249.8 57.7 %collective-permute-start.14 = (f32[64,128]{0,1:T(8,128)}, f32[64,128]{0,1:T(8,128)S(1)}, u32[]{:S(2)}, u32[]{:S(2)}) collective-permute-start(f32[64,128]{0,1:T(8,128)} %get-tuple-element.25), channel_id=1, source_target_pairs={{0,2},{2,4},{4,6},{6,8},{8,10},{10,12},{12,14},{14,16},{16,18},{18... | collective-permute-start | bytes 98312 | tf_op jit(solution)/shard_map/ppermute | solution.py:31
  254.3 53.9 %collective-permute-start.15 = (f32[64,128]{0,1:T(8,128)}, f32[64,128]{0,1:T(8,128)}, u32[]{:S(2)}, u32[]{:S(2)}) collective-permute-start(f32[64,128]{0,1:T(8,128)} %get-tuple-element.24), channel_id=1, source_target_pairs={{2,0},{4,2},{6,4},{8,6},{10,8},{12,10},{14,12},{16,14},{18,16},{20... | collective-permute-start | bytes 98312 | tf_op jit(solution)/shard_map/ppermute | solution.py:32
  333.3 56.6 %copy-start.47 = (f32[64]{0:T(128)S(1)}, f32[64]{0:T(128)}, u32[]{:S(2)}) copy-start(f32[64]{0:T(128)} %constant.32.clone) | copy-start | bytes 772
  333.3 58.9 %collective-permute-start.16 = (f32[64,128]{0,1:T(8,128)}, f32[64,128]{0,1:T(8,128)}, u32[]{:S(2)}, u32[]{:S(2)}) collective-permute-start(f32[64,128]{0,1:T(8,128)} %get-tuple-element.23), channel_id=1, source_target_pairs={{0,1},{2,3},{4,5},{6,7},{8,9},{10,11},{12,13},{14,15},{16,17},{18,... | collective-permute-start | bytes 98312 | tf_op jit(solution)/shard_map/ppermute | solution.py:31
  338.4 54.6 %collective-permute-start.17 = (f32[64,128]{0,1:T(8,128)}, f32[64,128]{0,1:T(8,128)S(1)}, u32[]{:S(2)}, u32[]{:S(2)}) collective-permute-start(f32[64,128]{0,1:T(8,128)} %get-tuple-element.22), channel_id=1, source_target_pairs={{1,0},{3,2},{5,4},{7,6},{9,8},{11,10},{13,12},{15,14},{17,16},{19,... | collective-permute-start | bytes 98312 | tf_op jit(solution)/shard_map/ppermute | solution.py:32
  339.7 53.4 %collective-permute-start.18 = (f32[64,128]{0,1:T(8,128)}, f32[64,128]{0,1:T(8,128)S(1)}, u32[]{:S(2)}, u32[]{:S(2)}) collective-permute-start(f32[64,128]{0,1:T(8,128)} %get-tuple-element.21), channel_id=1, source_target_pairs={{0,2},{2,4},{4,6},{6,8},{8,10},{10,12},{12,14},{14,16},{16,18},{18... | collective-permute-start | bytes 98312 | tf_op jit(solution)/shard_map/ppermute | solution.py:31
  343.7 49.4 %collective-permute-start.19 = (f32[64,128]{0,1:T(8,128)}, f32[64,128]{0,1:T(8,128)}, u32[]{:S(2)}, u32[]{:S(2)}) collective-permute-start(f32[64,128]{0,1:T(8,128)} %get-tuple-element.20), channel_id=1, source_target_pairs={{2,0},{4,2},{6,4},{8,6},{10,8},{12,10},{14,12},{16,14},{18,16},{20... | collective-permute-start | bytes 98312 | tf_op jit(solution)/shard_map/ppermute | solution.py:32
  (67 other events, 487.7 us)
where the time goes:
time: 413 us; the launch traced here: 407 us
  blocking collectives  178 us (43%)
  matrix products  82.6 us (20%)
  local copies, waits for them, and re-layouts  68.7 us (17%)
  starting transfers between devices  60.6 us (15%)
  other arithmetic  13.4 us (3%)
    psum x4, blocking collectives, outlet_totals(): return lax.psum(partial_value, ('region', 'sub'))  178 us
    ppermute x10, starting transfers between devices, extended(): before = lax.ppermute(last, axis, up)  47.2 us
    dot_general x5, matrix products, assemble(): jnp.einsum('vpq,qx->vpx', turner, fetched, precision=lax.Precision.HIGHEST)  21.6 us
    gather x5, local copies, waits for them, and re-layouts, assemble(): fetched = jnp.take(face_pool, jnp.minimum(links, limit - 1), axis=1)  20.8 us
    unnamed x164, local copies, waits for them, and re-layouts  18.3 us
    dot_general x9, matrix products, add_faces(): jnp.einsum('fqn,qfe->ne', selector, grouped, precision=lax.Precision.HIGH...  16.9 us
    ppermute x10, starting transfers between devices, extended(): after = lax.ppermute(first, axis, down)  13.3 us
    dot_general x9, matrix products, face_matrix(): jnp.einsum('fqn,ne->qfe', selector, flat_field, precision=lax.Precision.H...  12.7 us
  transfers between devices with their start and end apart: 20, of which 1 were waited for; matrix products, arithmetic and copies ran while one was open for 9% of the time, Pallas kernels for 0%

commit v1 on v0

--- a/solution.py
+++ b/solution.py
@@ -144,7 +144,7 @@
 def outlet_totals(direction, weights, area_flat, outlet_hits, selector):
     sums = jnp.dot(weights, face_matrix(direction, selector), precision=lax.Precision.HIGHEST)
     partial_value = jnp.dot(outlet_hits, area_flat * sums, precision=lax.Precision.HIGHEST)
-    return lax.psum(partial_value, ("region", "sub"))
+    return lax.psum(lax.psum(partial_value, "sub"), "region")
 
 
 def add_outlet(values, totals, weights, area_flat, outlet_hits, outlet_gain, selector):

time: 413 us -> 383 us (0.927)
  blocking collectives: 178 us -> 149 us
    psum x4 -> x8, blocking collectives: 178 us -> 149 us  [outlet_totals(): return lax.psum(lax.psum(partial_value, 'sub'), 'region')]
where the time goes in v1:
time: 383 us; the launch traced here: 377 us
  blocking collectives  149 us (39%)
  matrix products  82.6 us (22%)
  local copies, waits for them, and re-layouts  67.8 us (18%)
  starting transfers between devices  60.5 us (16%)
  other arithmetic  13.5 us (4%)
    psum x8, blocking collectives, outlet_totals(): return lax.psum(lax.psum(partial_value, 'sub'), 'region')  149 us
    ppermute x10, starting transfers between devices, extended(): before = lax.ppermute(last, axis, up)  46.5 us
    dot_general x5, matrix products, assemble(): jnp.einsum('vpq,qx->vpx', turner, fetched, precision=lax.Precision.HIGHEST)  21.6 us
    gather x5, local copies, waits for them, and re-layouts, assemble(): fetched = jnp.take(face_pool, jnp.minimum(links, limit - 1), axis=1)  20.8 us
    unnamed x164, local copies, waits for them, and re-layouts  17.4 us
    dot_general x9, matrix products, add_faces(): jnp.einsum('fqn,qfe->ne', selector, grouped, precision=lax.Precision.HIGH...  16.8 us
    ppermute x10, starting transfers between devices, extended(): after = lax.ppermute(first, axis, down)  14 us
    dot_general x9, matrix products, face_matrix(): jnp.einsum('fqn,ne->qfe', selector, flat_field, precision=lax.Precision.H...  12.8 us
  transfers between devices with their start and end apart: 20, of which 1 were waited for; matrix products, arithmetic and copies ran while one was open for 9% of the time, Pallas kernels for 0%

profile of v1, /device:TPU:0, one launch (start us, length us, event | category | flops | bytes accessed | tf_op | source)
XLA Modules:
  0.0 376.6 jit_solution(16202721161085297435)
XLA Ops:
  10.7 4.9 %collective-permute-start = (f32[64,128]{0,1:T(8,128)S(1)}, f32[64,128]{0,1:T(8,128)S(1)}, u32[]{:S(2)}, u32[]{:S(2)}) collective-permute-start(f32[64,128]{0,1:T(8,128)S(1)} %get-tuple-element.39), channel_id=1, source_target_pairs={{0,1},{2,3},{4,5},{6,7},{8,9},{10,11},{12,13},{14,15},{16,17},{18,... | collective-permute-start | bytes 98312 | tf_op jit(solution)/shard_map/ppermute | solution.py:31
  23.1 3.7 gather_fusion.1
  26.8 4.3 %fusion = f32[64,1536]{1,0:T(8,128)S(1)} fusion(f32[8,1536]{1,0:T(8,128)S(1)} %fusion.93, f32[8,64,64]{2,1,0:T(8,128)} %constant.59.clone, f32[1536,64]{1,0:T(8,128)} %gather_fusion.1, pred[1536]{0:T(1024)(128)(4,1)S(1)} %compare_and_fusion, pred[1536]{0:T(1024)(128)(4,1)S(1)} %lt.28), kind=kOutput, calls=%fused_computation.15 | convolution fusion | flops 605650944 | bytes 969728 | tf_op jit(solution)/shard_map/vpq,qx->vpx/dot_general | solution.py:139
  48.0 16.3 %collective-permute-start.4 = (f32[64,128]{0,1:T(8,128)}, f32[64,128]{0,1:T(8,128)}, u32[]{:S(2)}, u32[]{:S(2)}) collective-permute-start(f32[64,128]{0,1:T(8,128)} %get-tuple-element.35), channel_id=1, source_target_pairs={{0,1},{2,3},{4,5},{6,7},{8,9},{10,11},{12,13},{14,15},{16,17},{18,... | collective-permute-start | bytes 98312 | tf_op jit(solution)/shard_map/ppermute | solution.py:31
  68.0 5.2 %collective-permute-start.6 = (f32[64,128]{0,1:T(8,128)}, f32[64,128]{0,1:T(8,128)}, u32[]{:S(2)}, u32[]{:S(2)}) collective-permute-start(f32[64,128]{0,1:T(8,128)} %get-tuple-element.33), channel_id=1, source_target_pairs={{0,2},{2,4},{4,6},{6,8},{8,10},{10,12},{12,14},{14,16},{16,18},{18... | collective-permute-start | bytes 98312 | tf_op jit(solution)/shard_map/ppermute | solution.py:31
  73.2 5.2 %psum.56 = f32[8]{0:T(128)S(1)} all-reduce(f32[8]{0:T(128)S(1)} %convolution_bitcast_fusion.20), channel_id=1, replica_groups=mesh['region'=16,'sub'=2] {'sub'}, use_global_device_ids=true, to_apply=%region_2.5 | all-reduce | flops 8 | bytes 64 | tf_op jit(solution)/shard_map/psum | solution.py:147
  79.7 34.2 %psum.57 = f32[8]{0:T(128)S(1)} all-reduce(f32[8]{0:T(128)S(1)} %psum.56), channel_id=1, replica_groups=mesh['region'=16,'sub'=2] {'region'}, use_global_device_ids=true, to_apply=%region_3.6 | all-reduce | flops 8 | bytes 64 | tf_op jit(solution)/shard_map/psum | solution.py:147
  119.1 3.7 gather_fusion.3
  122.8 4.3 %fusion.1 = f32[64,1536]{1,0:T(8,128)S(1)} fusion(f32[8,1536]{1,0:T(8,128)S(1)} %copy-done.38, f32[8,64,64]{2,1,0:T(8,128)} %constant.59.clone, f32[1536,64]{1,0:T(8,128)} %gather_fusion.3, pred[1536]{0:T(1024)(128)(4,1)S(1)} %copy-done.60, pred[1536]{0:T(1024)(128)(4,1)S(1)} %copy-done.65), kind=kOutput, calls=%fused_computation.16 | convolution fusion | flops 605650944 | bytes 969728 | tf_op jit(solution)/shard_map/vpq,qx->vpx/dot_general | solution.py:139
  145.8 4.7 %collective-permute-start.8 = (f32[64,128]{0,1:T(8,128)}, f32[64,128]{0,1:T(8,128)}, u32[]{:S(2)}, u32[]{:S(2)}) collective-permute-start(f32[64,128]{0,1:T(8,128)} %get-tuple-element.31), channel_id=1, source_target_pairs={{0,1},{2,3},{4,5},{6,7},{8,9},{10,11},{12,13},{14,15},{16,17},{18,... | collective-permute-start | bytes 98312 | tf_op jit(solution)/shard_map/ppermute | solution.py:31
  154.9 5.5 %psum.58 = f32[8]{0:T(128)S(1)} all-reduce(f32[8]{0:T(128)S(1)} %convolution_bitcast_fusion.19), channel_id=1, replica_groups=mesh['region'=16,'sub'=2] {'sub'}, use_global_device_ids=true, to_apply=%region_5.8 | all-reduce | flops 8 | bytes 64 | tf_op jit(solution)/shard_map/psum | solution.py:147
  161.7 30.6 %psum.59 = f32[8]{0:T(128)S(1)} all-reduce(f32[8]{0:T(128)S(1)} %psum.58), channel_id=1, replica_groups=mesh['region'=16,'sub'=2] {'region'}, use_global_device_ids=true, to_apply=%region_6.9 | all-reduce | flops 8 | bytes 64 | tf_op jit(solution)/shard_map/psum | solution.py:147
  200.5 4.9 %gather_fusion.5 = f32[1536,64]{1,0:T(8,128)} fusion(f32[64,2048]{0,1:T(8,128)} %constant_dynamic-update-slice_fusion.10, s32[2048]{0:T(1024)S(1)} %pad_clamp_fusion), kind=kCustom, calls=%fused_computation.7.clone | custom fusion | bytes 792576 | tf_op jit(solution)/shard_map/jit(_take)/gather | solution.py:137
  205.4 4.3 %fusion.2 = f32[64,1536]{1,0:T(8,128)S(1)} fusion(f32[8,1536]{1,0:T(8,128)S(1)} %copy-done.38, f32[8,64,64]{2,1,0:T(8,128)} %constant.59.clone, f32[1536,64]{1,0:T(8,128)} %gather_fusion.5, pred[1536]{0:T(1024)(128)(4,1)S(1)} %copy-done.61, pred[1536]{0:T(1024)(128)(4,1)S(1)} %copy-done.66), kind=kOutput, calls=%fused_computation.17 | convolution fusion | flops 605650944 | bytes 969728 | tf_op jit(solution)/shard_map/vpq,qx->vpx/dot_general | solution.py:139
  228.9 4.7 %collective-permute-start.12 = (f32[64,128]{0,1:T(8,128)}, f32[64,128]{0,1:T(8,128)}, u32[]{:S(2)}, u32[]{:S(2)}) collective-permute-start(f32[64,128]{0,1:T(8,128)} %get-tuple-element.27), channel_id=1, source_target_pairs={{0,1},{2,3},{4,5},{6,7},{8,9},{10,11},{12,13},{14,15},{16,17},{18,... | collective-permute-start | bytes 98312 | tf_op jit(solution)/shard_map/ppermute | solution.py:31
  239.9 5.6 %psum.60 = f32[8]{0:T(128)S(1)} all-reduce(f32[8]{0:T(128)} %convolution_bitcast_fusion.18), channel_id=1, replica_groups=mesh['region'=16,'sub'=2] {'sub'}, use_global_device_ids=true, to_apply=%region_8.11 | all-reduce | flops 8 | bytes 64 | tf_op jit(solution)/shard_map/psum | solution.py:147
  246.9 31.1 %psum.61 = f32[8]{0:T(128)} all-reduce(f32[8]{0:T(128)S(1)} %psum.60), channel_id=1, replica_groups=mesh['region'=16,'sub'=2] {'region'}, use_global_device_ids=true, to_apply=%region_9.12 | all-reduce | flops 8 | bytes 64 | tf_op jit(solution)/shard_map/psum | solution.py:147
  288.4 4.9 %gather_fusion.7 = f32[1536,64]{1,0:T(8,128)} fusion(f32[64,2048]{0,1:T(8,128)} %constant_dynamic-update-slice_fusion.15, s32[2048]{0:T(1024)S(1)} %pad_clamp_fusion), kind=kCustom, calls=%fused_computation.8.clone | custom fusion | bytes 792576 | tf_op jit(solution)/shard_map/jit(_take)/gather | solution.py:137
  293.3 4.3 %fusion.3 = f32[64,1536]{1,0:T(8,128)S(1)} fusion(f32[8,1536]{1,0:T(8,128)S(1)} %copy-done.38, f32[8,64,64]{2,1,0:T(8,128)} %constant.59.clone, f32[1536,64]{1,0:T(8,128)} %gather_fusion.7, pred[1536]{0:T(1024)(128)(4,1)S(1)} %copy-done.62, pred[1536]{0:T(1024)(128)(4,1)S(1)} %copy-done.67), kind=kOutput, calls=%fused_computation.18 | convolution fusion | flops 605650944 | bytes 969728 | tf_op jit(solution)/shard_map/vpq,qx->vpx/dot_general | solution.py:139
  312.1 4.1 %collective-permute-start.16 = (f32[64,128]{0,1:T(8,128)}, f32[64,128]{0,1:T(8,128)S(1)}, u32[]{:S(2)}, u32[]{:S(2)}) collective-permute-start(f32[64,128]{0,1:T(8,128)} %get-tuple-element.23), channel_id=1, source_target_pairs={{0,1},{2,3},{4,5},{6,7},{8,9},{10,11},{12,13},{14,15},{16,17},{18,... | collective-permute-start | bytes 98312 | tf_op jit(solution)/shard_map/ppermute | solution.py:31
  322.1 5.5 %psum.62 = f32[8]{0:T(128)S(1)} all-reduce(f32[8]{0:T(128)S(1)} %convolution_bitcast_fusion.17), channel_id=1, replica_groups=mesh['region'=16,'sub'=2] {'sub'}, use_global_device_ids=true, to_apply=%region_11.14 | all-reduce | flops 8 | bytes 64 | tf_op jit(solution)/shard_map/psum | solution.py:147
  328.9 30.6 %psum.63 = f32[8]{0:T(128)S(1)} all-reduce(f32[8]{0:T(128)S(1)} %psum.62), channel_id=1, replica_groups=mesh['region'=16,'sub'=2] {'region'}, use_global_device_ids=true, to_apply=%region_12.15 | all-reduce | flops 8 | bytes 64 | tf_op jit(solution)/shard_map/psum | solution.py:147
  363.8 3.7 gather_fusion.9
  367.5 4.3 %fusion.4 = f32[64,1536]{1,0:T(8,128)S(1)} fusion(f32[8,1536]{1,0:T(8,128)S(1)} %copy-done.39, f32[8,64,64]{2,1,0:T(8,128)} %constant.59.clone, f32[1536,64]{1,0:T(8,128)} %gather_fusion.9, pred[1536]{0:T(1024)(128)(4,1)S(1)} %copy-done.63, pred[1536]{0:T(1024)(128)(4,1)S(1)} %copy-done.68), kind=kOutput, calls=%fused_computation.19 | convolution fusion | flops 605650944 | bytes 969728 | tf_op jit(solution)/shard_map/vpq,qx->vpx/dot_general | solution.py:139
  (329 shorter events, 143.3 us)
Async XLA Ops:
  10.7 11.4 %collective-permute-start = (f32[64,128]{0,1:T(8,128)S(1)}, f32[64,128]{0,1:T(8,128)S(1)}, u32[]{:S(2)}, u32[]{:S(2)}) collective-permute-start(f32[64,128]{0,1:T(8,128)S(1)} %get-tuple-element.39), channel_id=1, source_target_pairs={{0,1},{2,3},{4,5},{6,7},{8,9},{10,11},{12,13},{14,15},{16,17},{18,... | collective-permute-start | bytes 98312 | tf_op jit(solution)/shard_map/ppermute | solution.py:31
  15.6 6.5 %collective-permute-start.1 = (f32[64,128]{0,1:T(8,128)S(1)}, f32[64,128]{0,1:T(8,128)S(1)}, u32[]{:S(2)}, u32[]{:S(2)}) collective-permute-start(f32[64,128]{0,1:T(8,128)S(1)} %get-tuple-element.38), channel_id=1, source_target_pairs={{1,0},{3,2},{5,4},{7,6},{9,8},{11,10},{13,12},{15,14},{17,16},{19,... | collective-permute-start | bytes 98312 | tf_op jit(solution)/shard_map/ppermute | solution.py:32
  16.9 5.2 %collective-permute-start.2 = (f32[64,128]{0,1:T(8,128)S(1)}, f32[64,128]{0,1:T(8,128)S(1)}, u32[]{:S(2)}, u32[]{:S(2)}) collective-permute-start(f32[64,128]{0,1:T(8,128)S(1)} %get-tuple-element.37), channel_id=1, source_target_pairs={{0,2},{2,4},{4,6},{6,8},{8,10},{10,12},{12,14},{14,16},{16,18},{18... | collective-permute-start | bytes 98312 | tf_op jit(solution)/shard_map/ppermute | solution.py:31
  18.4 4.7 %collective-permute-start.3 = (f32[64,128]{0,1:T(8,128)S(1)}, f32[64,128]{0,1:T(8,128)S(1)}, u32[]{:S(2)}, u32[]{:S(2)}) collective-permute-start(f32[64,128]{0,1:T(8,128)S(1)} %get-tuple-element.36), channel_id=1, source_target_pairs={{2,0},{4,2},{6,4},{8,6},{10,8},{12,10},{14,12},{16,14},{18,16},{20... | collective-permute-start | bytes 98312 | tf_op jit(solution)/shard_map/ppermute | solution.py:32
  48.0 66.0 %copy-start.69 = (f32[8]{0:T(128)S(1)}, f32[8]{0:T(128)}, u32[]{:S(2)}) copy-start(f32[8]{0:T(128)} %param.19) | copy-start | bytes 100
  48.0 66.2 %copy-start.45 = (f32[64]{0:T(128)S(1)}, f32[64]{0:T(128)}, u32[]{:S(2)}) copy-start(f32[64]{0:T(128)} %constant.32.clone) | copy-start | bytes 772
  48.0 68.5 %collective-permute-start.4 = (f32[64,128]{0,1:T(8,128)}, f32[64,128]{0,1:T(8,128)}, u32[]{:S(2)}, u32[]{:S(2)}) collective-permute-start(f32[64,128]{0,1:T(8,128)} %get-tuple-element.35), channel_id=1, source_target_pairs={{0,1},{2,3},{4,5},{6,7},{8,9},{10,11},{12,13},{14,15},{16,17},{18,... | collective-permute-start | bytes 98312 | tf_op jit(solution)/shard_map/ppermute | solution.py:31
  64.3 53.1 %collective-permute-start.5 = (f32[64,128]{0,1:T(8,128)}, f32[64,128]{0,1:T(8,128)S(1)}, u32[]{:S(2)}, u32[]{:S(2)}) collective-permute-start(f32[64,128]{0,1:T(8,128)} %get-tuple-element.34), channel_id=1, source_target_pairs={{1,0},{3,2},{5,4},{7,6},{9,8},{11,10},{13,12},{15,14},{17,16},{19,... | collective-permute-start | bytes 98312 | tf_op jit(solution)/shard_map/ppermute | solution.py:32
  68.0 49.4 %collective-permute-start.6 = (f32[64,128]{0,1:T(8,128)}, f32[64,128]{0,1:T(8,128)}, u32[]{:S(2)}, u32[]{:S(2)}) collective-permute-start(f32[64,128]{0,1:T(8,128)} %get-tuple-element.33), channel_id=1, source_target_pairs={{0,2},{2,4},{4,6},{6,8},{8,10},{10,12},{12,14},{14,16},{16,18},{18... | collective-permute-start | bytes 98312 | tf_op jit(solution)/shard_map/ppermute | solution.py:31
  78.4 39.8 %collective-permute-start.7 = (f32[64,128]{0,1:T(8,128)}, f32[64,128]{0,1:T(8,128)}, u32[]{:S(2)}, u32[]{:S(2)}) collective-permute-start(f32[64,128]{0,1:T(8,128)} %get-tuple-element.32), channel_id=1, source_target_pairs={{2,0},{4,2},{6,4},{8,6},{10,8},{12,10},{14,12},{16,14},{18,16},{20... | collective-permute-start | bytes 98312 | tf_op jit(solution)/shard_map/ppermute | solution.py:32
  145.8 51.4 %collective-permute-start.8 = (f32[64,128]{0,1:T(8,128)}, f32[64,128]{0,1:T(8,128)}, u32[]{:S(2)}, u32[]{:S(2)}) collective-permute-start(f32[64,128]{0,1:T(8,128)} %get-tuple-element.31), channel_id=1, source_target_pairs={{0,1},{2,3},{4,5},{6,7},{8,9},{10,11},{12,13},{14,15},{16,17},{18,... | collective-permute-start | bytes 98312 | tf_op jit(solution)/shard_map/ppermute | solution.py:31
  150.5 48.1 %collective-permute-start.9 = (f32[64,128]{0,1:T(8,128)}, f32[64,128]{0,1:T(8,128)S(1)}, u32[]{:S(2)}, u32[]{:S(2)}) collective-permute-start(f32[64,128]{0,1:T(8,128)} %get-tuple-element.30), channel_id=1, source_target_pairs={{1,0},{3,2},{5,4},{7,6},{9,8},{11,10},{13,12},{15,14},{17,16},{19,... | collective-permute-start | bytes 98312 | tf_op jit(solution)/shard_map/ppermute | solution.py:32
  153.5 45.7 %collective-permute-start.10 = (f32[64,128]{0,1:T(8,128)}, f32[64,128]{0,1:T(8,128)S(1)}, u32[]{:S(2)}, u32[]{:S(2)}) collective-permute-start(f32[64,128]{0,1:T(8,128)} %get-tuple-element.29), channel_id=1, source_target_pairs={{0,2},{2,4},{4,6},{6,8},{8,10},{10,12},{12,14},{14,16},{16,18},{18... | collective-permute-start | bytes 98312 | tf_op jit(solution)/shard_map/ppermute | solution.py:31
  160.4 39.4 %collective-permute-start.11 = (f32[64,128]{0,1:T(8,128)}, f32[64,128]{0,1:T(8,128)S(1)}, u32[]{:S(2)}, u32[]{:S(2)}) collective-permute-start(f32[64,128]{0,1:T(8,128)} %get-tuple-element.28), channel_id=1, source_target_pairs={{2,0},{4,2},{6,4},{8,6},{10,8},{12,10},{14,12},{16,14},{18,16},{20... | collective-permute-start | bytes 98312 | tf_op jit(solution)/shard_map/ppermute | solution.py:32
  228.9 51.3 %copy-start.46 = (f32[64]{0:T(128)S(1)}, f32[64]{0:T(128)}, u32[]{:S(2)}) copy-start(f32[64]{0:T(128)} %constant.32.clone) | copy-start | bytes 772
  228.9 54.4 %collective-permute-start.12 = (f32[64,128]{0,1:T(8,128)}, f32[64,128]{0,1:T(8,128)}, u32[]{:S(2)}, u32[]{:S(2)}) collective-permute-start(f32[64,128]{0,1:T(8,128)} %get-tuple-element.27), channel_id=1, source_target_pairs={{0,1},{2,3},{4,5},{6,7},{8,9},{10,11},{12,13},{14,15},{16,17},{18,... | collective-permute-start | bytes 98312 | tf_op jit(solution)/shard_map/ppermute | solution.py:31
  233.6 51.2 %collective-permute-start.13 = (f32[64,128]{0,1:T(8,128)}, f32[64,128]{0,1:T(8,128)S(1)}, u32[]{:S(2)}, u32[]{:S(2)}) collective-permute-start(f32[64,128]{0,1:T(8,128)} %get-tuple-element.26), channel_id=1, source_target_pairs={{1,0},{3,2},{5,4},{7,6},{9,8},{11,10},{13,12},{15,14},{17,16},{19,... | collective-permute-start | bytes 98312 | tf_op jit(solution)/shard_map/ppermute | solution.py:32
  238.0 47.4 %collective-permute-start.14 = (f32[64,128]{0,1:T(8,128)}, f32[64,128]{0,1:T(8,128)}, u32[]{:S(2)}, u32[]{:S(2)}) collective-permute-start(f32[64,128]{0,1:T(8,128)} %get-tuple-element.25), channel_id=1, source_target_pairs={{0,2},{2,4},{4,6},{6,8},{8,10},{10,12},{12,14},{14,16},{16,18},{18... | collective-permute-start | bytes 98312 | tf_op jit(solution)/shard_map/ppermute | solution.py:31
  245.6 41.3 %collective-permute-start.15 = (f32[64,128]{0,1:T(8,128)}, f32[64,128]{0,1:T(8,128)}, u32[]{:S(2)}, u32[]{:S(2)}) collective-permute-start(f32[64,128]{0,1:T(8,128)} %get-tuple-element.24), channel_id=1, source_target_pairs={{2,0},{4,2},{6,4},{8,6},{10,8},{12,10},{14,12},{16,14},{18,16},{20... | collective-permute-start | bytes 98312 | tf_op jit(solution)/shard_map/ppermute | solution.py:32
  312.1 47.6 %copy-start.47 = (f32[64]{0:T(128)S(1)}, f32[64]{0:T(128)}, u32[]{:S(2)}) copy-start(f32[64]{0:T(128)} %constant.32.clone) | copy-start | bytes 772
  312.1 49.9 %collective-permute-start.16 = (f32[64,128]{0,1:T(8,128)}, f32[64,128]{0,1:T(8,128)S(1)}, u32[]{:S(2)}, u32[]{:S(2)}) collective-permute-start(f32[64,128]{0,1:T(8,128)} %get-tuple-element.23), channel_id=1, source_target_pairs={{0,1},{2,3},{4,5},{6,7},{8,9},{10,11},{12,13},{14,15},{16,17},{18,... | collective-permute-start | bytes 98312 | tf_op jit(solution)/shard_map/ppermute | solution.py:31
  316.2 45.8 %collective-permute-start.17 = (f32[64,128]{0,1:T(8,128)}, f32[64,128]{0,1:T(8,128)S(1)}, u32[]{:S(2)}, u32[]{:S(2)}) collective-permute-start(f32[64,128]{0,1:T(8,128)} %get-tuple-element.22), channel_id=1, source_target_pairs={{1,0},{3,2},{5,4},{7,6},{9,8},{11,10},{13,12},{15,14},{17,16},{19,... | collective-permute-start | bytes 98312 | tf_op jit(solution)/shard_map/ppermute | solution.py:32
  320.2 41.9 %collective-permute-start.18 = (f32[64,128]{0,1:T(8,128)}, f32[64,128]{0,1:T(8,128)}, u32[]{:S(2)}, u32[]{:S(2)}) collective-permute-start(f32[64,128]{0,1:T(8,128)} %get-tuple-element.21), channel_id=1, source_target_pairs={{0,2},{2,4},{4,6},{6,8},{8,10},{10,12},{12,14},{14,16},{16,18},{18... | collective-permute-start | bytes 98312 | tf_op jit(solution)/shard_map/ppermute | solution.py:31
  327.6 35.3 %collective-permute-start.19 = (f32[64,128]{0,1:T(8,128)}, f32[64,128]{0,1:T(8,128)}, u32[]{:S(2)}, u32[]{:S(2)}) collective-permute-start(f32[64,128]{0,1:T(8,128)} %get-tuple-element.20), channel_id=1, source_target_pairs={{2,0},{4,2},{6,4},{8,6},{10,8},{12,10},{14,12},{16,14},{18,16},{20... | collective-permute-start | bytes 98312 | tf_op jit(solution)/shard_map/ppermute | solution.py:32
  (67 other events, 449.3 us)
